TPU v7x, 32 devices: a whole 2x2x4 slice. The times are simulated.
32 devices in a mesh: dp: 16 (over z, x, core), seq: 2 (over y).
Axes of the slice: x: 2, y: 2, z: 4, core: 2. Of those that a mesh axis runs over, the one named last changes fastest.
Arguments:
- character_codes: int32 [16, 512, 50], P('dp', 'seq'), may hold values from 0 to 262
- word_lengths: int32 [16, 512], P('dp', 'seq'), may hold values from 1 to 50
- sequence_lengths: int32 [16], P('dp'), may hold values from 128 to 512, as said below
- character_table: bfloat16 [263, 16], replicated, may hold values from -6 to 6
- conv_width1: bfloat16 [16, 32], replicated, may hold values from -1.5 to 1.5
- conv_width2: bfloat16 [32, 32], replicated, may hold values from -1 to 1
- conv_width3: bfloat16 [48, 64], replicated, may hold values from -0.875 to 0.875
- conv_width4: bfloat16 [64, 128], replicated, may hold values from -0.75 to 0.75
- conv_width5: bfloat16 [80, 256], replicated, may hold values from -0.625 to 0.625
- conv_width6: bfloat16 [96, 512], replicated, may hold values from -0.625 to 0.625
- conv_width7: bfloat16 [112, 1024], replicated, may hold values from -0.5 to 0.5
- conv_bias: bfloat16 [2048], replicated, may hold values from -2.5 to -0.5
- highway_weight: bfloat16 [2048, 4096], P('dp'), may hold values from -0.125 to 0.125
- highway_bias: bfloat16 [4096], replicated, may hold values from -5 to 5
- projection: bfloat16 [2048, 768], P('dp'), may hold values from -0.125 to 0.125
- position_table: bfloat16 [512, 768], replicated, may hold values from -6 to 6
- attention_in: bfloat16 [768, 2304], P('dp'), may hold values from -0.3125 to 0.3125
- attention_out: bfloat16 [768, 768], P('dp'), may hold values from -0.875 to 0.875
- norm1_gain: bfloat16 [768], replicated, may hold values from 0.5 to 1.5
- norm1_bias: bfloat16 [768], replicated, may hold values from -1.5 to 1.5
- hidden_in: bfloat16 [768, 3072], P('dp'), may hold values from -0.21875 to 0.21875
- hidden_out: bfloat16 [3072, 768], P('dp'), may hold values from -0.15625 to 0.15625
- norm2_gain: bfloat16 [768], replicated, may hold values from 0.5 to 1.5
- norm2_bias: bfloat16 [768], replicated, may hold values from -1.5 to 1.5
- cotangent: bfloat16 [16, 512, 768], P('dp', 'seq'), may hold values from -6 to 6
Outputs:
- layer_out: bfloat16 [16, 512, 768], P('dp', 'seq')
- character_table_gradient: float32 [263, 16], replicated
- conv_width1_gradient: float32 [16, 32], replicated
- conv_width2_gradient: float32 [32, 32], replicated
- conv_width3_gradient: float32 [48, 64], replicated
- conv_width4_gradient: float32 [64, 128], replicated
- conv_width5_gradient: float32 [80, 256], replicated
- conv_width6_gradient: float32 [96, 512], replicated
- conv_width7_gradient: float32 [112, 1024], replicated
- conv_bias_gradient: float32 [2048], replicated
- highway_weight_gradient: float32 [2048, 4096], P('dp')
- highway_bias_gradient: float32 [4096], replicated
- projection_gradient: float32 [2048, 768], P('dp')
- position_table_gradient: float32 [512, 768], replicated
- attention_in_gradient: float32 [768, 2304], P('dp')
- attention_out_gradient: float32 [768, 768], P('dp')
- norm1_gain_gradient: float32 [768], replicated
- norm1_bias_gradient: float32 [768], replicated
- hidden_in_gradient: float32 [768, 3072], P('dp')
- hidden_out_gradient: float32 [3072, 768], P('dp')
- norm2_gain_gradient: float32 [768], replicated
- norm2_bias_gradient: float32 [768], replicated
Inputs may be any that keep to these rules, and one draw needn't show every extreme that they name: `sequence_lengths`: keys at or after a sequence's length take no part in attention; the first sequence has all 512 words.
All inputs are finite; a program needn't handle non-finite values.
Results may differ from a plain program's by a relative error of at most 0.028.
The roundings to bfloat16 on the way count: a program that leaves them out, or rounds other values in their place, can miss the bound.
Values may be sent and summed in bfloat16 or wider, within the bound.
No kernel may reach another device: no remote copies, remote signals or barrier semaphores. Data moves between devices by JAX's collectives and lax.ppermute only.
A program may use at most 256 MiB of HBM per device.

v0:
```python
from functools import partial
import math
import jax
import jax.numpy as jnp
from jax import lax
from jax.sharding import PartitionSpec as P

HEAD_DIM = 64
exact_gelu = partial(jax.nn.gelu, approximate=False)


def layer_norm(value, gain, bias):
    mean = jnp.mean(value, axis=-1, keepdims=True)
    centered = value - mean
    spread = jnp.mean(centered * centered, axis=-1, keepdims=True)
    return centered * lax.rsqrt(spread + 1e-12) * gain + bias


def highway_mix(gates, hidden):
    filters = hidden.shape[1]
    carry = jax.nn.sigmoid(gates[:, filters:])
    return carry * hidden + (1.0 - carry) * jax.nn.relu(gates[:, :filters])


def character_maps(codes, lengths, table, kernels):
    vocab = table.shape[0]
    features = table.shape[1]
    letters = codes.shape[1]
    onehot = (codes[:, :, None] == jnp.arange(vocab, dtype=jnp.int32)[None, None, :]).astype(
        jnp.bfloat16
    )
    embed = jnp.einsum("wcv,ve->wce", onehot, table, preferred_element_type=jnp.float32).astype(
        jnp.bfloat16
    )
    maps = []
    for kernel in kernels:
        width = kernel.shape[0] // features
        count = letters - width + 1
        window = jnp.concatenate(
            [embed[:, shift : shift + count] for shift in range(width)], axis=2
        )
        conv = jnp.einsum("wpk,kc->wpc", window, kernel, preferred_element_type=jnp.float32)
        limit = jnp.maximum(lengths - width + 1, 1)
        valid = jnp.arange(count, dtype=jnp.int32)[None, :] < limit[:, None]
        maps.append((window, jnp.where(valid[:, :, None], conv, -1e30)))
    return (onehot, maps)


def character_pool(codes, lengths, table, kernels):
    onehot, maps = character_maps(codes, lengths, table, kernels)
    return jnp.concatenate([jnp.max(entry[1], axis=1) for entry in maps], axis=1)


def character_back(codes, lengths, grad_block, table, kernels):
    onehot, maps = character_maps(codes, lengths, table, kernels)
    features = table.shape[1]
    letters = codes.shape[1]
    grad_embed = jnp.zeros((codes.shape[0], letters, features), jnp.float32)
    kernel_grads = []
    offset = 0
    for kernel, entry in zip(kernels, maps):
        window, masked = entry
        width = kernel.shape[0] // features
        channels = kernel.shape[1]
        count = letters - width + 1
        top = jnp.max(masked, axis=1, keepdims=True)
        hits = (masked == top).astype(jnp.float32)
        share = (
            grad_block[:, None, offset : offset + channels]
            * hits
            / jnp.sum(hits, axis=1, keepdims=True)
        )
        share = share.astype(jnp.bfloat16)
        offset = offset + channels
        kernel_grads.append(
            jnp.einsum("wpk,wpc->kc", window, share, preferred_element_type=jnp.float32)
        )
        grad_window = jnp.einsum("wpc,kc->wpk", share, kernel, preferred_element_type=jnp.float32)
        for shift in range(width):
            piece = grad_window[:, :, shift * features : (shift + 1) * features]
            grad_embed = grad_embed + jnp.pad(
                piece, ((0, 0), (shift, letters - count - shift), (0, 0))
            )
    table_grad = jnp.einsum(
        "wcv,wce->ve", onehot, grad_embed.astype(jnp.bfloat16), preferred_element_type=jnp.float32
    )
    return (tuple(kernel_grads), table_grad)


def score_heads(query_heads, key_heads, keep):
    raw = (
        jnp.einsum("qhd,khd->hqk", query_heads, key_heads, preferred_element_type=jnp.float32)
        * 0.125
    )
    return jnp.where(keep[None, None, :], raw, -1e30)


def body(
    character_codes,
    word_lengths,
    sequence_lengths,
    character_table,
    conv_width1,
    conv_width2,
    conv_width3,
    conv_width4,
    conv_width5,
    conv_width6,
    conv_width7,
    conv_bias,
    highway_weight,
    highway_bias,
    projection,
    position_table,
    attention_in,
    attention_out,
    norm1_gain,
    norm1_bias,
    hidden_in,
    hidden_out,
    norm2_gain,
    norm2_bias,
    cotangent,
):
    kernels = (
        conv_width1,
        conv_width2,
        conv_width3,
        conv_width4,
        conv_width5,
        conv_width6,
        conv_width7,
    )
    highway_full, projection_full = (
        lax.all_gather(highway_weight, "dp", axis=0, tiled=True),
        lax.all_gather(projection, "dp", axis=0, tiled=True),
    )
    codes = character_codes[0]
    lengths = word_lengths[0]
    words = codes.shape[0]
    letters = codes.shape[1]
    block = math.gcd(words, 32)
    code_blocks = codes.reshape(words // block, block, letters)
    length_blocks = lengths.reshape(words // block, block)
    pooled = lax.map(
        lambda pair: character_pool(pair[0], pair[1], character_table, kernels),
        (code_blocks, length_blocks),
    )
    pooled = pooled.reshape(words, pooled.shape[2])
    biased = pooled + conv_bias.astype(jnp.float32)
    hidden0 = jax.nn.relu(biased)
    hidden0_low = hidden0.astype(jnp.bfloat16)
    attention_full, output_full, inward_full, outward_full = (
        lax.all_gather(attention_in, "dp", axis=0, tiled=True),
        lax.all_gather(attention_out, "dp", axis=0, tiled=True),
        lax.all_gather(hidden_in, "dp", axis=0, tiled=True),
        lax.all_gather(hidden_out, "dp", axis=0, tiled=True),
    )
    gates = jnp.dot(
        hidden0_low, highway_full, preferred_element_type=jnp.float32
    ) + highway_bias.astype(jnp.float32)
    hidden1 = highway_mix(gates, hidden0)
    hidden1_low = hidden1.astype(jnp.bfloat16)
    offset = lax.axis_index("seq") * words
    positions = lax.dynamic_slice_in_dim(position_table, offset, words, 0).astype(jnp.float32)
    embedded = jnp.dot(hidden1_low, projection_full, preferred_element_type=jnp.float32) + positions
    embedded_low = embedded.astype(jnp.bfloat16)
    model = embedded.shape[1]
    heads = model // HEAD_DIM
    projected = jnp.dot(embedded_low, attention_full, preferred_element_type=jnp.float32).astype(
        jnp.bfloat16
    )
    gathered = lax.all_gather(projected[:, model:], "seq", axis=0, tiled=True)
    length = gathered.shape[0]
    query_heads = projected[:, :model].reshape(words, heads, HEAD_DIM)
    key_heads = gathered[:, :model].reshape(length, heads, HEAD_DIM)
    value_heads = gathered[:, model:].reshape(length, heads, HEAD_DIM)
    keep = jnp.arange(length, dtype=jnp.int32) < sequence_lengths[0]
    scores = score_heads(query_heads, key_heads, keep)
    top = jnp.max(scores, axis=-1, keepdims=True)
    unnormalized = jnp.exp(scores - top)
    total = jnp.sum(unnormalized, axis=-1, keepdims=True)
    probs_low = (unnormalized / total).astype(jnp.bfloat16)
    attended = jnp.einsum(
        "hqk,khd->qhd", probs_low, value_heads, preferred_element_type=jnp.float32
    )
    attended = attended.reshape(words, model).astype(jnp.bfloat16)
    joined = embedded + jnp.dot(attended, output_full, preferred_element_type=jnp.float32)
    gain1 = norm1_gain.astype(jnp.float32)
    shift1 = norm1_bias.astype(jnp.float32)
    gain2 = norm2_gain.astype(jnp.float32)
    shift2 = norm2_bias.astype(jnp.float32)
    normed1 = layer_norm(joined, gain1, shift1)
    normed1_low = normed1.astype(jnp.bfloat16)
    inner = jnp.dot(normed1_low, inward_full, preferred_element_type=jnp.float32)
    active = exact_gelu(inner).astype(jnp.bfloat16)
    summed = normed1 + jnp.dot(active, outward_full, preferred_element_type=jnp.float32)
    layer_out = layer_norm(summed, gain2, shift2).astype(jnp.bfloat16)
    seed_grad = cotangent[0].astype(jnp.float32)
    _, norm2_pull = jax.vjp(layer_norm, summed, gain2, shift2)
    grad_summed, norm2_gain_grad, norm2_bias_grad = norm2_pull(seed_grad)
    grad_outer = grad_summed.astype(jnp.bfloat16)
    hidden_out_grad = jnp.einsum(
        "tf,td->fd", active, grad_outer, preferred_element_type=jnp.float32
    )
    grad_active = jnp.einsum(
        "td,fd->tf", grad_outer, outward_full, preferred_element_type=jnp.float32
    )
    _, gelu_pull = jax.vjp(exact_gelu, inner)
    grad_inner = gelu_pull(grad_active)[0].astype(jnp.bfloat16)
    hidden_in_grad = jnp.einsum(
        "td,tf->df", normed1_low, grad_inner, preferred_element_type=jnp.float32
    )
    grad_normed1 = grad_summed + jnp.einsum(
        "tf,df->td", grad_inner, inward_full, preferred_element_type=jnp.float32
    )
    _, norm1_pull = jax.vjp(layer_norm, joined, gain1, shift1)
    grad_joined, norm1_gain_grad, norm1_bias_grad = norm1_pull(grad_normed1)
    grad_branch = grad_joined.astype(jnp.bfloat16)
    attention_out_grad = jnp.einsum(
        "td,te->de", attended, grad_branch, preferred_element_type=jnp.float32
    )
    grad_attended = jnp.einsum(
        "te,de->td", grad_branch, output_full, preferred_element_type=jnp.float32
    ).astype(jnp.bfloat16)
    grad_heads = grad_attended.reshape(words, heads, HEAD_DIM)
    probs = jnp.exp(score_heads(query_heads, key_heads, keep) - top) / total
    probs_again = probs.astype(jnp.bfloat16)
    grad_probs = jnp.einsum(
        "qhd,khd->hqk", grad_heads, value_heads, preferred_element_type=jnp.float32
    )
    grad_scores = (
        probs * (grad_probs - jnp.sum(probs * grad_probs, axis=-1, keepdims=True))
    ).astype(jnp.bfloat16)
    grad_query = (
        jnp.einsum("hqk,khd->qhd", grad_scores, key_heads, preferred_element_type=jnp.float32)
        * 0.125
    )
    count = lax.axis_size("seq") * words
    score_part = lax.slice_in_dim(grad_scores, 0, count, axis=2)
    prob_part = lax.slice_in_dim(probs_again, 0, count, axis=2)
    key_grad = (
        jnp.einsum("hqk,qhd->khd", score_part, query_heads, preferred_element_type=jnp.float32)
        * 0.125
    )
    value_grad = jnp.einsum(
        "hqk,qhd->khd", prob_part, grad_heads, preferred_element_type=jnp.float32
    )
    grad_pairs = lax.psum_scatter(
        jnp.concatenate(
            [key_grad.reshape(count, model), value_grad.reshape(count, model)], axis=1
        ).astype(jnp.bfloat16),
        "seq",
        scatter_dimension=0,
        tiled=True,
    ).astype(jnp.float32)
    grad_projected = jnp.concatenate([grad_query.reshape(words, model), grad_pairs], axis=1).astype(
        jnp.bfloat16
    )
    attention_in_grad = jnp.einsum(
        "td,te->de", embedded_low, grad_projected, preferred_element_type=jnp.float32
    )
    grad_embedded = grad_joined + jnp.einsum(
        "te,de->td", grad_projected, attention_full, preferred_element_type=jnp.float32
    )
    position_grad = lax.dynamic_update_slice_in_dim(
        jnp.zeros((length, model), jnp.float32), grad_embedded, offset, 0
    )
    grad_mapped = grad_embedded.astype(jnp.bfloat16)
    projection_grad = jnp.einsum(
        "tf,td->fd", hidden1_low, grad_mapped, preferred_element_type=jnp.float32
    )
    grad_hidden1 = jnp.einsum(
        "td,fd->tf", grad_mapped, projection_full, preferred_element_type=jnp.float32
    )
    _, highway_pull = jax.vjp(highway_mix, gates, hidden0)
    grad_gates, grad_carry = highway_pull(grad_hidden1)
    grad_gates = grad_gates.astype(jnp.bfloat16)
    highway_grad = jnp.einsum(
        "tf,tg->fg", hidden0_low, grad_gates, preferred_element_type=jnp.float32
    )
    highway_bias_grad = jnp.sum(grad_gates.astype(jnp.float32), axis=0)
    grad_hidden0 = grad_carry + jnp.einsum(
        "tg,fg->tf", grad_gates, highway_full, preferred_element_type=jnp.float32
    )
    grad_pooled = jnp.where(biased > 0, grad_hidden0, 0.0)
    conv_bias_grad = jnp.sum(grad_pooled, axis=0)
    grad_blocks = grad_pooled.reshape(words // block, block, grad_pooled.shape[1])

    def conv_step(carry, item):
        kernel_sum, table_sum = carry
        kernel_part, table_part = character_back(
            item[0], item[1], item[2], character_table, kernels
        )
        return ((jax.tree.map(jnp.add, kernel_sum, kernel_part), table_sum + table_part), None)

    start_sums = (
        tuple((jnp.zeros(kernel.shape, jnp.float32) for kernel in kernels)),
        jnp.zeros(character_table.shape, jnp.float32),
    )
    sums, _ = lax.scan(conv_step, start_sums, (code_blocks, length_blocks, grad_blocks))
    kernel_grads, table_grad = sums
    share_highway, share_projection, share_attention, share_output, share_inward, share_outward = (
        lax.psum_scatter(highway_grad, "dp", scatter_dimension=0, tiled=True),
        lax.psum_scatter(projection_grad, "dp", scatter_dimension=0, tiled=True),
        lax.psum_scatter(attention_in_grad, "dp", scatter_dimension=0, tiled=True),
        lax.psum_scatter(attention_out_grad, "dp", scatter_dimension=0, tiled=True),
        lax.psum_scatter(hidden_in_grad, "dp", scatter_dimension=0, tiled=True),
        lax.psum_scatter(hidden_out_grad, "dp", scatter_dimension=0, tiled=True),
    )
    highway_total, projection_total, attention_total, output_total, inward_total, outward_total = (
        lax.psum(share_highway.astype(jnp.bfloat16), "seq").astype(jnp.float32),
        lax.psum(share_projection.astype(jnp.bfloat16), "seq").astype(jnp.float32),
        lax.psum(share_attention.astype(jnp.bfloat16), "seq").astype(jnp.float32),
        lax.psum(share_output.astype(jnp.bfloat16), "seq").astype(jnp.float32),
        lax.psum(share_inward.astype(jnp.bfloat16), "seq").astype(jnp.float32),
        lax.psum(share_outward.astype(jnp.bfloat16), "seq").astype(jnp.float32),
    )
    small = lax.psum(
        (
            table_grad,
            kernel_grads[0],
            kernel_grads[1],
            kernel_grads[2],
            kernel_grads[3],
            kernel_grads[4],
            kernel_grads[5],
            kernel_grads[6],
            conv_bias_grad,
            highway_bias_grad,
            position_grad,
            norm1_gain_grad,
            norm1_bias_grad,
            norm2_gain_grad,
            norm2_bias_grad,
        ),
        ("dp", "seq"),
    )
    return (
        layer_out[None],
        small[0],
        small[1],
        small[2],
        small[3],
        small[4],
        small[5],
        small[6],
        small[7],
        small[8],
        highway_total,
        small[9],
        projection_total,
        small[10],
        attention_total,
        output_total,
        small[11],
        small[12],
        inward_total,
        outward_total,
        small[13],
        small[14],
    )


def solution(mesh):
    placed = (
        P("dp", "seq", None),
        P("dp", "seq"),
        P("dp"),
        P(),
        P(),
        P(),
        P(),
        P(),
        P(),
        P(),
        P(),
        P(),
        P("dp", None),
        P(),
        P("dp", None),
        P(),
        P("dp", None),
        P("dp", None),
        P(),
        P(),
        P("dp", None),
        P("dp", None),
        P(),
        P(),
        P("dp", "seq", None),
    )
    return jax.shard_map(
        body,
        mesh=mesh,
        in_specs=placed,
        out_specs=(
            P("dp", "seq", None),
            P(),
            P(),
            P(),
            P(),
            P(),
            P(),
            P(),
            P(),
            P(),
            P("dp", None),
            P(),
            P("dp", None),
            P(),
            P("dp", None),
            P("dp", None),
            P(),
            P(),
            P("dp", None),
            P("dp", None),
            P(),
            P(),
        ),
        check_vma=False,
    )
```

profile of v0, /device:TPU:0, one launch (start us, length us, event | category | flops | bytes accessed | tf_op | source)
XLA Modules:
  0.0 2102.8 jit_solution(11255074296748637753)
XLA Ops:
  14.3 119.6 %while.43 = (s32[]{:T(128)}, f32[8,32,2048]{2,1,0:T(8,128)S(1)}, s32[8,32]{1,0:T(8,128)}, s32[8,32,50]{2,1,0:T(8,128)}, bf16[263,16]{0,1:T(8,128)(2,1)}, /*index...) while((s32[]{:T(128)}, f32[8,32,2048]{2,1,0:T(8,128)S(1)}, ...), condition=%wide.region_8.9_spmd, body=%wide.region_0.8_spmd.sunk | while | flops 584907392 | bytes 8470321 | solution.py:145
  134.3 5.5 all-gather.8.cloned.1.call-done
  139.8 8.1 convolution_add_fusion.1
  150.8 34.9 %all-gather.10.cloned.1.call-done = bf16[2048,768]{1,0:T(8,128)(2,1)} async-done(((bf16[128,768]{1,0:T(8,128)(2,1)}), bf16[2048,768]{1,0:T(8,128)(2,1)}) %all-gather.10.cloned.1.call-update) | async-done | bytes 3145744 | tf_op jit(solution)/shard_map/all_gather | solution.py:136
  188.6 45.3 %all-gather.12.cloned.1.call-done = bf16[768,2304]{1,0:T(8,128)(2,1)} async-done(((bf16[48,2304]{1,0:T(8,128)(2,1)}), bf16[768,2304]{1,0:T(8,128)(2,1)}) %all-gather.12.cloned.1.call-update) | async-done | bytes 3538960 | tf_op jit(solution)/shard_map/all_gather | solution.py:154
  244.8 20.6 all-gather.14.cloned.1.call-done
  267.5 5.5 fusion.317
  273.0 4.0 fusion.246
  277.0 28.9 %all-gather.16.cloned.1.call-done = bf16[768,768]{1,0:T(8,128)(2,1)} async-done(((bf16[48,768]{1,0:T(8,128)(2,1)}), bf16[768,768]{1,0:T(8,128)(2,1)}) %all-gather.16.cloned.1.call-update) | async-done | bytes 1179664 | tf_op jit(solution)/shard_map/all_gather | solution.py:155
  308.1 52.2 %all-gather.18.cloned.1.call-done = bf16[768,3072]{1,0:T(8,128)(2,1)} async-done(((bf16[48,3072]{1,0:T(8,128)(2,1)}), bf16[768,3072]{1,0:T(8,128)(2,1)}) %all-gather.18.cloned.1.call-update) | async-done | bytes 4718608 | tf_op jit(solution)/shard_map/all_gather | solution.py:156
  360.3 11.2 multiply_convert_fusion.1
  371.5 42.9 %all-gather.20.cloned.1.call-done = bf16[3072,768]{1,0:T(8,128)(2,1)} async-done(((bf16[192,768]{1,0:T(8,128)(2,1)}), bf16[3072,768]{1,0:T(8,128)(2,1)}) %all-gather.20.cloned.1.call-update) | async-done | bytes 4718608 | tf_op jit(solution)/shard_map/all_gather | solution.py:157
  414.5 4.0 fusion.319
  443.9 18.5 reduce-scatter.8.cloned.1.call-done
  463.6 4.7 constant_dynamic-update-slice_fusion
  474.4 4.1 fusion.255
  480.2 5.2 fusion.275
  487.0 5.1 fusion.272
  493.7 7.2 fusion.231
  502.9 13.8 fusion.279
  518.3 12.3 fusion.320
  532.1 85.6 %reduce-scatter.12.cloned.1.call-done = f32[128,768]{1,0:T(8,128)} async-done(((f32[2048,768]{1,0:T(8,128)}), f32[128,768]{1,0:T(8,128)}) %reduce-scatter.12.cloned.1.call-update) | async-done | bytes 393232 | tf_op jit(solution)/shard_map/reduce_scatter | solution.py:305
  619.4 92.0 %reduce-scatter.14.cloned.1.call-done = f32[48,2304]{1,0:T(8,128)} async-done(((f32[768,2304]{1,0:T(8,128)}), f32[48,2304]{1,0:T(8,128)}) %reduce-scatter.14.cloned.1.call-update) | async-done | bytes 442384 | tf_op jit(solution)/shard_map/reduce_scatter | solution.py:306
  713.1 113.1 %reduce-scatter.18.cloned.1.call-done = f32[48,3072]{1,0:T(8,128)} async-done(((f32[768,3072]{1,0:T(8,128)}), f32[48,3072]{1,0:T(8,128)}) %reduce-scatter.18.cloned.1.call-update) | async-done | bytes 589840 | tf_op jit(solution)/shard_map/reduce_scatter | solution.py:308
  828.1 114.0 %reduce-scatter.20.cloned.1.call-done = f32[192,768]{1,0:T(8,128)} async-done(((f32[3072,768]{1,0:T(8,128)}), f32[192,768]{1,0:T(8,128)}) %reduce-scatter.20.cloned.1.call-update) | async-done | bytes 589840 | tf_op jit(solution)/shard_map/reduce_scatter | solution.py:309
  943.9 334.8 %reduce-scatter.10.cloned.1.call-done = f32[128,4096]{1,0:T(8,128)} async-done(((f32[2048,4096]{1,0:T(8,128)}), f32[128,4096]{1,0:T(8,128)}) %reduce-scatter.10.cloned.1.call-update) | async-done | bytes 2097168 | tf_op jit(solution)/shard_map/reduce_scatter | solution.py:304
  1281.4 518.9 %while.44 = (s32[]{:T(128)}, f32[16,32]{1,0:T(8,128)}, f32[32,32]{1,0:T(8,128)}, f32[48,64]{1,0:T(8,128)}, f32[64,128]{1,0:T(8,128)}, /*index=5*/f32[80,256]{1,0...) while((s32[]{:T(128)}, f32[16,32]{1,0:T(8,128)}, ...), condition=%wide.region_36.37_spmd.clone, body=%wide.region_21.36_spmd.clone.sunk | while | flops 1773396992 | bytes 44253568 | solution.py:301
  1310.4 4.7 convert_reduce_fusion.22
  1332.2 3.8 fusion.513
  1337.9 5.0 fusion.515
  1375.7 4.7 convert_reduce_fusion.22
  1397.6 3.8 fusion.513
  1403.3 5.0 fusion.515
  1441.1 4.7 convert_reduce_fusion.22
  1468.6 5.0 fusion.515
  1506.4 4.7 convert_reduce_fusion.22
  1534.0 5.0 fusion.515
  1571.7 4.7 convert_reduce_fusion.22
  1593.6 3.8 fusion.513
  1599.3 5.0 fusion.515
  1637.1 4.7 convert_reduce_fusion.22
  1664.7 5.0 fusion.515
  1702.4 4.7 convert_reduce_fusion.22
  1730.0 5.0 fusion.515
  1767.8 4.7 convert_reduce_fusion.22
  1795.4 5.0 fusion.515
  1810.9 119.0 %all-reduce.36.cloned.1.call-done = (f32[263,16]{0,1:T(8,128)}, f32[16,32]{1,0:T(8,128)}, f32[32,32]{1,0:T(8,128)}, f32[48,64]{1,0:T(8,128)}, f32[64,128]{1,0:T(...) async-done(((f32[263,16]{0,1:T(8,128)}, f32[16,32]{1,0:T(8,128)}, f32[32,32]{1,0:T(8,128)}, ...) | async-done | bytes 104912 | tf_op jit(solution)/shard_map/psum | solution.py:319
  1929.9 146.9 %all-reduce.38.cloned.1.call-done = (f32[80,256]{1,0:T(8,128)}, f32[96,512]{1,0:T(8,128)}, f32[112,1024]{1,0:T(8,128)}, f32[512,768]{1,0:T(8,128)}) async-done(((f32[80,256]{1,0:T(8,128)}, f32[96,512]{1,0:T(8,128)}, f32[112,1024]{1,0:T(8,128)}, f32[512,768]{1,0:T(8,128)}), (f32[80,256]{1,0:T(8,128)}, f32[96,512]{1,0:T(8,128)}, f32[112,1024]{1,0:T(8,128)}, ...) | async-done | bytes 2310160 | tf_op jit(solution)/shard_map/psum | solution.py:319
  (1530 shorter events, 652.7 us)
Async XLA Ops:
  7.2 132.6 %all-gather.8.cloned.1.call-start = ((), (), s32[]{:S(2)}) async-start(), calls=%async_computation.7 | async-start | bytes 17825792 | tf_op jit(solution)/shard_map/all_gather | solution.py:135
  7.9 177.7 %all-gather.10.cloned.1.call-start = ((), (), s32[]{:S(2)}) async-start(), calls=%async_computation.8 | async-start | bytes 3342336 | tf_op jit(solution)/shard_map/all_gather | solution.py:136
  8.7 225.3 %all-gather.12.cloned.1.call-start = ((), (), s32[]{:S(2)}) async-start(), calls=%async_computation.9 | async-start | bytes 3760128 | tf_op jit(solution)/shard_map/all_gather | solution.py:154
  9.4 256.0 %all-gather.14.cloned.1.call-start = ((), (), s32[]{:S(2)}) async-start(), calls=%async_computation.10 | async-start | bytes 2359296 | tf_op jit(solution)/shard_map/all_gather | solution.py:173
  14.3 119.7 %copy-start.68 = (bf16[2048]{0:T(1024)(128)(2,1)S(1)}, bf16[2048]{0:T(1024)(128)(2,1)}, u32[]{:S(2)}) copy-start(bf16[2048]{0:T(1024)(128)(2,1)} %param.40) | copy-start | bytes 12292
  14.3 119.7 %copy-start.65 = (bf16[4096]{0:T(1024)(128)(2,1)S(1)}, bf16[4096]{0:T(1024)(128)(2,1)}, u32[]{:S(2)}) copy-start(bf16[4096]{0:T(1024)(128)(2,1)} %param.42) | copy-start | bytes 24580
  134.0 14.0 copy-start.2
  150.8 86.3 %copy-start.8 = (bf16[256,2048]{1,0:T(8,128)(2,1)}, bf16[256,2048]{1,0:T(8,128)(2,1)S(1)}, u32[]{:S(2)}) copy-start(bf16[256,2048]{1,0:T(8,128)(2,1)S(1)} %fusion.230) | copy-start | bytes 3145732
  188.6 117.4 %copy-start.19 = (f32[256,768]{1,0:T(8,128)}, f32[256,768]{1,0:T(8,128)S(1)}, u32[]{:S(2)}) copy-start(f32[256,768]{1,0:T(8,128)S(1)} %convolution_add_fusion.7) | copy-start | bytes 2359300
  188.6 53.3 %copy-start.73 = (bf16[768]{0:T(1024)(128)(2,1)S(1)}, bf16[768]{0:T(1024)(128)(2,1)}, u32[]{:S(2)}) copy-start(bf16[768]{0:T(1024)(128)(2,1)} %param.48) | copy-start | bytes 4612
  188.6 53.3 %copy-start.74 = (bf16[768]{0:T(1024)(128)(2,1)S(1)}, bf16[768]{0:T(1024)(128)(2,1)}, u32[]{:S(2)}) copy-start(bf16[768]{0:T(1024)(128)(2,1)} %param.47) | copy-start | bytes 4612
  188.6 53.3 %copy-start.75 = (bf16[768]{0:T(1024)(128)(2,1)S(1)}, bf16[768]{0:T(1024)(128)(2,1)}, u32[]{:S(2)}) copy-start(bf16[768]{0:T(1024)(128)(2,1)} %param.51) | copy-start | bytes 4612
  188.6 53.9 %copy-start.76 = (bf16[768]{0:T(1024)(128)(2,1)S(1)}, bf16[768]{0:T(1024)(128)(2,1)}, u32[]{:S(2)}) copy-start(bf16[768]{0:T(1024)(128)(2,1)} %param.52) | copy-start | bytes 4612
  239.1 66.9 %all-gather.16.cloned.1.call-start = ((), (), s32[]{:S(2)}) async-start(), calls=%async_computation.11 | async-start | bytes 1253376 | tf_op jit(solution)/shard_map/all_gather | solution.py:155
  239.7 120.6 %all-gather.18.cloned.1.call-start = ((), (), s32[]{:S(2)}) async-start(), calls=%async_computation.12 | async-start | bytes 5013504 | tf_op jit(solution)/shard_map/all_gather | solution.py:156
  240.2 174.2 %all-gather.20.cloned.1.call-start = ((), (), s32[]{:S(2)}) async-start(), calls=%async_computation.13 | async-start | bytes 5013504 | tf_op jit(solution)/shard_map/all_gather | solution.py:157
  241.0 221.4 %reduce-scatter.8.cloned.1.call-start = ((), (), s32[]{:S(2)}) async-start(), calls=%async_computation.14 | async-start | bytes 2359296 | tf_op jit(solution)/shard_map/reduce_scatter | solution.py:249
  244.8 22.7 %copy-start.26 = (bf16[256,768]{0,1:T(8,128)(2,1)}, bf16[256,768]{0,1:T(8,128)(2,1)S(1)}, u32[]{:S(2)}) copy-start(bf16[256,768]{0,1:T(8,128)(2,1)S(1)} %copy.248) | copy-start | bytes 1179652
  277.0 31.1 %copy-start.30 = (bf16[12,64,256]{2,1,0:T(8,128)(2,1)}, bf16[12,64,256]{2,1,0:T(8,128)(2,1)S(1)}, u32[]{:S(2)}) copy-start(bf16[12,64,256]{2,1,0:T(8,128)(2,1)S(1)} %fusion.246) | copy-start | bytes 1179652
  307.8 117.4 %copy-start = (f32[256,768]{1,0:T(8,128)}, f32[256,768]{1,0:T(8,128)S(1)}, u32[]{:S(2)}) copy-start(f32[256,768]{1,0:T(8,128)S(1)} %get-tuple-element.978) | copy-start | bytes 2359300
  307.8 106.6 %copy-start.52 = (f32[256]{0:T(256)}, f32[256]{0:T(256)S(1)}, u32[]{:S(2)}) copy-start(f32[256]{0:T(256)S(1)} %broadcast_multiply_fusion.1) | copy-start | bytes 3076
  308.0 63.4 %copy-start.62 = (f32[256]{0:T(256)}, f32[256]{0:T(256)S(1)}, u32[]{:S(2)}) copy-start(f32[256]{0:T(256)S(1)} %multiply_reduce_fusion.4) | copy-start | bytes 3076
  308.1 106.3 %copy-start.59 = (f32[256]{0:T(256)}, f32[256]{0:T(256)S(1)}, u32[]{:S(2)}) copy-start(f32[256]{0:T(256)S(1)} %fusion.266) | copy-start | bytes 3076
  371.5 47.0 %copy-start.22 = (bf16[256,3072]{1,0:T(8,128)(2,1)}, bf16[256,3072]{1,0:T(8,128)(2,1)S(1)}, u32[]{:S(2)}) copy-start(bf16[256,3072]{1,0:T(8,128)(2,1)S(1)} %get-tuple-element.896) | copy-start | bytes 4718596
  414.4 6.4 slice-start.6
  414.4 6.4 slice-start.7
  427.9 6.4 slice-start.2
  437.6 93.0 %reduce-scatter.16.cloned.1.call-start = ((), (), s32[]{:S(2)}) async-start(), calls=%async_computation.18 | async-start | bytes 2506752 | tf_op jit(solution)/shard_map/reduce_scatter | solution.py:307
  440.9 176.8 %reduce-scatter.12.cloned.1.call-start = ((), (), s32[]{:S(2)}) async-start(), calls=%async_computation.16 | async-start | bytes 6684672 | tf_op jit(solution)/shard_map/reduce_scatter | solution.py:305
  472.8 238.6 %reduce-scatter.14.cloned.1.call-start = ((), (), s32[]{:S(2)}) async-start(), calls=%async_computation.17 | async-start | bytes 7520256 | tf_op jit(solution)/shard_map/reduce_scatter | solution.py:306
  478.5 347.8 %reduce-scatter.18.cloned.1.call-start = ((), (), s32[]{:S(2)}) async-start(), calls=%async_computation.19 | async-start | bytes 10027008 | tf_op jit(solution)/shard_map/reduce_scatter | solution.py:308
  485.4 456.7 %reduce-scatter.20.cloned.1.call-start = ((), (), s32[]{:S(2)}) async-start(), calls=%async_computation.20 | async-start | bytes 10027008 | tf_op jit(solution)/shard_map/reduce_scatter | solution.py:309
  492.1 10.8 copy-start.11
  492.1 786.5 %reduce-scatter.10.cloned.1.call-start = ((), (), s32[]{:S(2)}) async-start(), calls=%async_computation.15 | async-start | bytes 35651584 | tf_op jit(solution)/shard_map/reduce_scatter | solution.py:304
  516.7 1287.3 %all-reduce.40.cloned.1.call-start = ((), (), s32[]{:S(2)}) async-start(), calls=%async_computation.23 | async-start | bytes 4259840 | tf_op jit(solution)/shard_map/psum | solution.py:312
  1281.4 648.5 %all-reduce.36.cloned.1.call-start = ((), (), s32[]{:S(2)}) async-start(), calls=%async_computation.21 | async-start | bytes 294912 | tf_op jit(solution)/shard_map/psum | solution.py:319
  1362.0 7.3 copy-start.79
  1427.4 7.3 copy-start.79
  1492.7 7.3 copy-start.79
  1558.1 7.3 copy-start.79
  1623.4 7.3 copy-start.79
  1688.8 7.3 copy-start.79
  1754.1 7.3 copy-start.79
  1803.4 273.3 %all-reduce.38.cloned.1.call-start = ((), (), s32[]{:S(2)}) async-start(), calls=%async_computation.22 | async-start | bytes 4620288 | tf_op jit(solution)/shard_map/psum | solution.py:319
  1929.9 163.8 %copy-start.72 = (f32[768]{0:T(1024)S(1)}, f32[768]{0:T(1024)}, u32[]{:S(2)}) copy-start(f32[768]{0:T(1024)} %get-tuple-element.1457) | copy-start | bytes 9220
  1929.9 164.4 %copy-start.71 = (f32[768]{0:T(1024)S(1)}, f32[768]{0:T(1024)}, u32[]{:S(2)}) copy-start(f32[768]{0:T(1024)} %get-tuple-element.1458) | copy-start | bytes 9220
  1929.9 165.0 %copy-start.70 = (f32[768]{0:T(1024)S(1)}, f32[768]{0:T(1024)}, u32[]{:S(2)}) copy-start(f32[768]{0:T(1024)} %get-tuple-element.1461) | copy-start | bytes 9220
  1929.9 165.6 %copy-start.69 = (f32[768]{0:T(1024)S(1)}, f32[768]{0:T(1024)}, u32[]{:S(2)}) copy-start(f32[768]{0:T(1024)} %get-tuple-element.1462) | copy-start | bytes 9220
  (252 other events, 636.0 us)
Sparse Core Ops, SparseCore 0:
  10.2 129.5 all-gather.7
  142.1 43.5 all-gather.9
  187.9 45.9 all-gather.11
  239.2 26.2 all-gather.13
  267.6 38.3 all-gather.15
  308.1 52.1 all-gather.17
  362.6 51.7 all-gather.19
  437.7 24.6 reduce-scatter.7
  466.6 62.9 reduce-scatter.15
  533.4 84.2 reduce-scatter.11
  622.2 89.1 reduce-scatter.13
  715.4 110.8 reduce-scatter.17
  830.9 111.1 reduce-scatter.19
  946.2 332.4 reduce-scatter.9
  1282.3 63.6 all-reduce.39
  1803.6 126.2 all-reduce.35
  1938.0 138.7 all-reduce.37
where the time goes:
time: 2120 us; the launch traced here: 2100 us
  waiting for transfers between devices  1260 us (59%)
  matrix products  601 us (28%)
  local copies, waits for them, and re-layouts  170 us (8%)
  other arithmetic  51.1 us (2%)
    reduce_scatter x1, waiting for transfers between devices, body(): lax.psum_scatter(highway_grad, 'dp', scatter_dimension=0, tiled=True)  335 us
    psum x2, waiting for transfers between devices, body(): lax.psum((table_grad, kernel_grads[0], kernel_grads[1], kernel_grads[2],...  266 us
    dot_general x56, matrix products, character_back(): jnp.einsum('wpk,wpc->kc', window, share, preferred_element_type=jnp.float32)  131 us
    eq x56, matrix products, character_back(): hits = (masked == top).astype(jnp.float32)  116 us
    reduce_scatter x1, waiting for transfers between devices, body(): lax.psum_scatter(hidden_out_grad, 'dp', scatter_dimension=0, tiled=True)  114 us
    reduce_scatter x1, waiting for transfers between devices, body(): lax.psum_scatter(hidden_in_grad, 'dp', scatter_dimension=0, tiled=True)  113 us
    dot_general x48, matrix products, character_back(): jnp.einsum('wpc,kc->wpk', share, kernel, preferred_element_type=jnp.float32)  103 us
    reduce_scatter x1, waiting for transfers between devices, body(): lax.psum_scatter(attention_in_grad, 'dp', scatter_dimension=0, tiled=True)  92 us
  transfers between devices with their start and end apart: 17, of which 15 were waited for; matrix products, arithmetic and copies ran while one was open for 35% of the time, Pallas kernels for 0%

commit v1 on v0

--- a/solution.py
+++ b/solution.py
@@ -317,24 +317,27 @@
         lax.psum(share_outward.astype(jnp.bfloat16), "seq").astype(jnp.float32),
     )
     small = lax.psum(
-        (
-            table_grad,
-            kernel_grads[0],
-            kernel_grads[1],
-            kernel_grads[2],
-            kernel_grads[3],
-            kernel_grads[4],
-            kernel_grads[5],
-            kernel_grads[6],
-            conv_bias_grad,
-            highway_bias_grad,
-            position_grad,
-            norm1_gain_grad,
-            norm1_bias_grad,
-            norm2_gain_grad,
-            norm2_bias_grad,
+        lax.psum(
+            (
+                table_grad,
+                kernel_grads[0],
+                kernel_grads[1],
+                kernel_grads[2],
+                kernel_grads[3],
+                kernel_grads[4],
+                kernel_grads[5],
+                kernel_grads[6],
+                conv_bias_grad,
+                highway_bias_grad,
+                position_grad,
+                norm1_gain_grad,
+                norm1_bias_grad,
+                norm2_gain_grad,
+                norm2_bias_grad,
+            ),
+            "seq",
         ),
-        ("dp", "seq"),
+        "dp",
     )
     return (
         layer_out[None],

time: 2120 us -> 1690 us (0.80)
  waiting for transfers between devices: 1260 us -> 825 us
    psum x0 -> x2, waiting for transfers between devices: none -> 193 us  [body(): lax.psum(lax.psum((table_grad, kernel_grads[0], kernel_grads[1], kernel_g...]
    psum x2, waiting for transfers between devices: 266 us -> 96 us  [body(): lax.psum((table_grad, kernel_grads[0], kernel_grads[1], kernel_grads[2],...]
    reduce_scatter x1, waiting for transfers between devices: 335 us -> 214 us  [body(): lax.psum_scatter(highway_grad, 'dp', scatter_dimension=0, tiled=True)]
    reduce_scatter x1, waiting for transfers between devices: 114 us -> 0.01 us  [body(): lax.psum_scatter(hidden_out_grad, 'dp', scatter_dimension=0, tiled=True)]
    reduce_scatter x1, waiting for transfers between devices: 113 us -> 0.01 us  [body(): lax.psum_scatter(hidden_in_grad, 'dp', scatter_dimension=0, tiled=True)]
    reduce_scatter x1, waiting for transfers between devices: 92 us -> 0.01 us  [body(): lax.psum_scatter(attention_in_grad, 'dp', scatter_dimension=0, tiled=True)]
    reduce_scatter x1, waiting for transfers between devices: 85.6 us -> 0.01 us  [body(): lax.psum_scatter(projection_grad, 'dp', scatter_dimension=0, tiled=True)]
    psum x1, waiting for transfers between devices: 0.02 us -> 68.1 us  [body(): lax.psum(share_highway.astype(jnp.bfloat16), 'seq').astype(jnp.float32)]
  transfers between devices with their start and end apart: 17 -> 19, of which waited for: 15 -> 14; matrix products, arithmetic and copies ran while one was open for 35% -> 44% of each run, Pallas kernels for 0% -> 0%
where the time goes in v1:
time: 1690 us; the launch traced here: 1670 us
  waiting for transfers between devices  825 us (49%)
  matrix products  603 us (36%)
  local copies, waits for them, and re-layouts  170 us (10%)
  other arithmetic  51.1 us (3%)
    reduce_scatter x1, waiting for transfers between devices, body(): lax.psum_scatter(highway_grad, 'dp', scatter_dimension=0, tiled=True)  214 us
    psum x2, waiting for transfers between devices, body(): lax.psum(lax.psum((table_grad, kernel_grads[0], kernel_grads[1], kernel_g...  193 us
    dot_general x56, matrix products, character_back(): jnp.einsum('wpk,wpc->kc', window, share, preferred_element_type=jnp.float32)  132 us
    eq x56, matrix products, character_back(): hits = (masked == top).astype(jnp.float32)  116 us
    dot_general x48, matrix products, character_back(): jnp.einsum('wpc,kc->wpk', share, kernel, preferred_element_type=jnp.float32)  103 us
    psum x2, waiting for transfers between devices, body(): lax.psum((table_grad, kernel_grads[0], kernel_grads[1], kernel_grads[2],...  96 us
    dot_general x56, matrix products, character_maps(): jnp.einsum('wpk,kc->wpc', window, kernel, preferred_element_type=jnp.floa...  69.8 us
    psum x1, waiting for transfers between devices, body(): lax.psum(share_highway.astype(jnp.bfloat16), 'seq').astype(jnp.float32)  68.1 us
  transfers between devices with their start and end apart: 19, of which 14 were waited for; matrix products, arithmetic and copies ran while one was open for 44% of the time, Pallas kernels for 0%

profile of v1, /device:TPU:0, one launch (start us, length us, event | category | flops | bytes accessed | tf_op | source)
XLA Modules:
  0.0 1671.9 jit_solution(8775266861976742508)
XLA Ops:
  14.3 119.6 %while.43 = (s32[]{:T(128)}, f32[8,32,2048]{2,1,0:T(8,128)S(1)}, s32[8,32]{1,0:T(8,128)}, s32[8,32,50]{2,1,0:T(8,128)}, bf16[263,16]{0,1:T(8,128)(2,1)}, /*index...) while((s32[]{:T(128)}, f32[8,32,2048]{2,1,0:T(8,128)S(1)}, ...), condition=%wide.region_8.9_spmd, body=%wide.region_0.8_spmd.sunk | while | flops 584907392 | bytes 8470321 | solution.py:145
  134.3 5.5 all-gather.8.cloned.1.call-done
  139.8 8.1 convolution_add_fusion.1
  150.8 34.9 %all-gather.10.cloned.1.call-done = bf16[2048,768]{1,0:T(8,128)(2,1)} async-done(((bf16[128,768]{1,0:T(8,128)(2,1)}), bf16[2048,768]{1,0:T(8,128)(2,1)}) %all-gather.10.cloned.1.call-update) | async-done | bytes 3145744 | tf_op jit(solution)/shard_map/all_gather | solution.py:136
  188.6 45.3 %all-gather.12.cloned.1.call-done = bf16[768,2304]{1,0:T(8,128)(2,1)} async-done(((bf16[48,2304]{1,0:T(8,128)(2,1)}), bf16[768,2304]{1,0:T(8,128)(2,1)}) %all-gather.12.cloned.1.call-update) | async-done | bytes 3538960 | tf_op jit(solution)/shard_map/all_gather | solution.py:154
  244.9 20.6 %all-gather.14.cloned.1.call-done = bf16[512,1536]{1,0:T(8,128)(2,1)} async-done(((bf16[256,1536]{1,0:T(8,128)(2,1)}), bf16[512,1536]{1,0:T(8,128)(2,1)}) %all-gather.14.cloned.1.call-update) | async-done | bytes 1572880 | tf_op jit(solution)/shard_map/all_gather | solution.py:173
  267.5 5.5 fusion.317
  273.0 4.0 fusion.246
  277.0 28.9 %all-gather.16.cloned.1.call-done = bf16[768,768]{1,0:T(8,128)(2,1)} async-done(((bf16[48,768]{1,0:T(8,128)(2,1)}), bf16[768,768]{1,0:T(8,128)(2,1)}) %all-gather.16.cloned.1.call-update) | async-done | bytes 1179664 | tf_op jit(solution)/shard_map/all_gather | solution.py:155
  308.1 52.2 %all-gather.18.cloned.1.call-done = bf16[768,3072]{1,0:T(8,128)(2,1)} async-done(((bf16[48,3072]{1,0:T(8,128)(2,1)}), bf16[768,3072]{1,0:T(8,128)(2,1)}) %all-gather.18.cloned.1.call-update) | async-done | bytes 4718608 | tf_op jit(solution)/shard_map/all_gather | solution.py:156
  360.3 11.2 multiply_convert_fusion.1
  371.5 42.9 %all-gather.20.cloned.1.call-done = bf16[3072,768]{1,0:T(8,128)(2,1)} async-done(((bf16[192,768]{1,0:T(8,128)(2,1)}), bf16[3072,768]{1,0:T(8,128)(2,1)}) %all-gather.20.cloned.1.call-update) | async-done | bytes 4718608 | tf_op jit(solution)/shard_map/all_gather | solution.py:157
  414.5 4.0 fusion.319
  443.9 18.5 %reduce-scatter.8.cloned.1.call-done = bf16[256,1536]{0,1:T(8,128)(2,1)} async-done(((bf16[512,1536]{0,1:T(8,128)(2,1)}), bf16[256,1536]{0,1:T(8,128)(2,1)}) %reduce-scatter.8.cloned.1.call-update) | async-done | bytes 786448 | tf_op jit(solution)/shard_map/reduce_scatter | solution.py:249
  463.6 4.7 constant_dynamic-update-slice_fusion
  473.6 4.1 fusion.255
  479.3 5.2 fusion.275
  486.2 5.0 fusion.272
  492.9 7.2 fusion.231
  502.1 13.8 fusion.279
  517.5 12.2 fusion.320
  529.8 522.5 %while.44 = (s32[]{:T(128)}, f32[16,32]{1,0:T(8,128)}, f32[32,32]{1,0:T(8,128)}, f32[48,64]{1,0:T(8,128)}, f32[64,128]{1,0:T(8,128)}, /*index=5*/f32[80,256]{1,0...) while((s32[]{:T(128)}, f32[16,32]{1,0:T(8,128)}, ...), condition=%wide.region_36.37_spmd.clone, body=%wide.region_21.36_spmd.clone.sunk | while | flops 1773396992 | bytes 44253568 | solution.py:301
  558.7 4.7 convert_reduce_fusion.22
  586.3 5.0 fusion.515
  624.1 4.7 convert_reduce_fusion.22
  628.9 4.0 fusion.502
  652.0 5.3 fusion.515
  690.1 4.7 convert_reduce_fusion.22
  717.7 5.0 fusion.515
  755.6 4.7 convert_reduce_fusion.22
  783.3 5.1 fusion.515
  821.2 4.7 convert_reduce_fusion.22
  843.1 3.9 fusion.513
  848.9 5.4 fusion.515
  887.1 4.7 convert_reduce_fusion.22
  914.8 5.0 fusion.515
  952.6 4.7 convert_reduce_fusion.22
  957.3 4.2 fusion.502
  975.0 3.9 fusion.513
  981.0 5.8 fusion.515
  1019.6 4.7 convert_reduce_fusion.22
  1047.3 5.0 fusion.515
  1064.6 214.1 %reduce-scatter.10.cloned.1.call-done = f32[128,4096]{1,0:T(8,128)} async-done(((f32[2048,4096]{1,0:T(8,128)}), f32[128,4096]{1,0:T(8,128)}) %reduce-scatter.10.cloned.1.call-update) | async-done | bytes 2097168 | tf_op jit(solution)/shard_map/reduce_scatter | solution.py:304
  1281.5 24.4 %all-reduce.44.cloned.1.call-done = (f32[263,16]{0,1:T(8,128)}, f32[16,32]{1,0:T(8,128)}, f32[32,32]{1,0:T(8,128)}, f32[48,64]{1,0:T(8,128)}, f32[64,128]{1,0:T(...) async-done(((f32[263,16]{0,1:T(8,128)}, f32[16,32]{1,0:T(8,128)}, f32[32,32]{1,0:T(8,128)}, ...) | async-done | bytes 104912 | tf_op jit(solution)/shard_map/psum | solution.py:320
  1306.0 71.5 %all-reduce.46.cloned.1.call-done = (f32[80,256]{1,0:T(8,128)}, f32[96,512]{1,0:T(8,128)}, f32[112,1024]{1,0:T(8,128)}, f32[512,768]{1,0:T(8,128)}) async-done(((f32[80,256]{1,0:T(8,128)}, f32[96,512]{1,0:T(8,128)}, f32[112,1024]{1,0:T(8,128)}, f32[512,768]{1,0:T(8,128)}), (f32[80,256]{1,0:T(8,128)}, f32[96,512]{1,0:T(8,128)}, f32[112,1024]{1,0:T(8,128)}, ...) | async-done | bytes 2310160 | tf_op jit(solution)/shard_map/psum | solution.py:320
  1377.5 68.1 %all-reduce.48.cloned.1.call-done = (bf16[128,4096]{1,0:T(8,128)(2,1)}, bf16[128,768]{1,0:T(8,128)(2,1)}, bf16[48,2304]{1,0:T(8,128)(2,1)}, bf16[48,768]{1,0:T(8...) async-done(((bf16[128,4096]{1,0:T(8,128)(2,1)}, bf16[128,768]{1,0:T(8,128)(2,1)}, bf16[48,2304]{1,0:T(8,128)(2,1)}, bf16[48,768]{1,0:T(8,128)(2,1)}, ...) | async-done | bytes 2129936 | tf_op jit(solution)/shard_map/psum | solution.py:312
  1452.5 88.8 %all-reduce.40.cloned.1.call-done = (f32[263,16]{0,1:T(8,128)}, f32[16,32]{1,0:T(8,128)}, f32[32,32]{1,0:T(8,128)}, f32[48,64]{1,0:T(8,128)}, f32[64,128]{1,0:T(...) async-done(((f32[263,16]{0,1:T(8,128)}, f32[16,32]{1,0:T(8,128)}, f32[32,32]{1,0:T(8,128)}, ...) | async-done | bytes 104912 | tf_op jit(solution)/shard_map/psum | solution.py:319
  1541.3 104.5 %all-reduce.42.cloned.1.call-done = (f32[80,256]{1,0:T(8,128)}, f32[96,512]{1,0:T(8,128)}, f32[112,1024]{1,0:T(8,128)}, f32[512,768]{1,0:T(8,128)}) async-done(((f32[80,256]{1,0:T(8,128)}, f32[96,512]{1,0:T(8,128)}, f32[112,1024]{1,0:T(8,128)}, f32[512,768]{1,0:T(8,128)}), (f32[80,256]{1,0:T(8,128)}, f32[96,512]{1,0:T(8,128)}, f32[112,1024]{1,0:T(8,128)}, ...) | async-done | bytes 2310160 | tf_op jit(solution)/shard_map/psum | solution.py:319
  (1534 shorter events, 649.7 us)
Async XLA Ops:
  7.2 132.6 %all-gather.8.cloned.1.call-start = ((), (), s32[]{:S(2)}) async-start(), calls=%async_computation.7 | async-start | bytes 17825792 | tf_op jit(solution)/shard_map/all_gather | solution.py:135
  7.9 177.7 %all-gather.10.cloned.1.call-start = ((), (), s32[]{:S(2)}) async-start(), calls=%async_computation.8 | async-start | bytes 3342336 | tf_op jit(solution)/shard_map/all_gather | solution.py:136
  8.7 225.3 %all-gather.12.cloned.1.call-start = ((), (), s32[]{:S(2)}) async-start(), calls=%async_computation.9 | async-start | bytes 3760128 | tf_op jit(solution)/shard_map/all_gather | solution.py:154
  9.4 256.0 %all-gather.14.cloned.1.call-start = ((), (), s32[]{:S(2)}) async-start(), calls=%async_computation.10 | async-start | bytes 2359296 | tf_op jit(solution)/shard_map/all_gather | solution.py:173
  14.3 119.7 %copy-start.67 = (bf16[2048]{0:T(1024)(128)(2,1)S(1)}, bf16[2048]{0:T(1024)(128)(2,1)}, u32[]{:S(2)}) copy-start(bf16[2048]{0:T(1024)(128)(2,1)} %param.40) | copy-start | bytes 12292
  14.3 119.7 %copy-start.64 = (bf16[4096]{0:T(1024)(128)(2,1)S(1)}, bf16[4096]{0:T(1024)(128)(2,1)}, u32[]{:S(2)}) copy-start(bf16[4096]{0:T(1024)(128)(2,1)} %param.42) | copy-start | bytes 24580
  134.0 14.0 copy-start.2
  150.7 86.3 %copy-start.8 = (bf16[256,2048]{1,0:T(8,128)(2,1)}, bf16[256,2048]{1,0:T(8,128)(2,1)S(1)}, u32[]{:S(2)}) copy-start(bf16[256,2048]{1,0:T(8,128)(2,1)S(1)} %fusion.230) | copy-start | bytes 3145732
  188.6 117.4 %copy-start.19 = (f32[256,768]{1,0:T(8,128)}, f32[256,768]{1,0:T(8,128)S(1)}, u32[]{:S(2)}) copy-start(f32[256,768]{1,0:T(8,128)S(1)} %convolution_add_fusion.7) | copy-start | bytes 2359300
  188.6 53.3 %copy-start.72 = (bf16[768]{0:T(1024)(128)(2,1)S(1)}, bf16[768]{0:T(1024)(128)(2,1)}, u32[]{:S(2)}) copy-start(bf16[768]{0:T(1024)(128)(2,1)} %param.48) | copy-start | bytes 4612
  188.6 53.3 %copy-start.73 = (bf16[768]{0:T(1024)(128)(2,1)S(1)}, bf16[768]{0:T(1024)(128)(2,1)}, u32[]{:S(2)}) copy-start(bf16[768]{0:T(1024)(128)(2,1)} %param.47) | copy-start | bytes 4612
  188.6 53.3 %copy-start.74 = (bf16[768]{0:T(1024)(128)(2,1)S(1)}, bf16[768]{0:T(1024)(128)(2,1)}, u32[]{:S(2)}) copy-start(bf16[768]{0:T(1024)(128)(2,1)} %param.51) | copy-start | bytes 4612
  188.6 53.9 %copy-start.75 = (bf16[768]{0:T(1024)(128)(2,1)S(1)}, bf16[768]{0:T(1024)(128)(2,1)}, u32[]{:S(2)}) copy-start(bf16[768]{0:T(1024)(128)(2,1)} %param.52) | copy-start | bytes 4612
  239.1 66.9 %all-gather.16.cloned.1.call-start = ((), (), s32[]{:S(2)}) async-start(), calls=%async_computation.11 | async-start | bytes 1253376 | tf_op jit(solution)/shard_map/all_gather | solution.py:155
  239.7 120.6 %all-gather.18.cloned.1.call-start = ((), (), s32[]{:S(2)}) async-start(), calls=%async_computation.12 | async-start | bytes 5013504 | tf_op jit(solution)/shard_map/all_gather | solution.py:156
  240.2 174.2 %all-gather.20.cloned.1.call-start = ((), (), s32[]{:S(2)}) async-start(), calls=%async_computation.13 | async-start | bytes 5013504 | tf_op jit(solution)/shard_map/all_gather | solution.py:157
  241.0 221.4 %reduce-scatter.8.cloned.1.call-start = ((), (), s32[]{:S(2)}) async-start(), calls=%async_computation.14 | async-start | bytes 2359296 | tf_op jit(solution)/shard_map/reduce_scatter | solution.py:249
  244.8 22.7 %copy-start.26 = (bf16[256,768]{0,1:T(8,128)(2,1)}, bf16[256,768]{0,1:T(8,128)(2,1)S(1)}, u32[]{:S(2)}) copy-start(bf16[256,768]{0,1:T(8,128)(2,1)S(1)} %copy.248) | copy-start | bytes 1179652
  277.0 31.1 %copy-start.30 = (bf16[12,64,256]{2,1,0:T(8,128)(2,1)}, bf16[12,64,256]{2,1,0:T(8,128)(2,1)S(1)}, u32[]{:S(2)}) copy-start(bf16[12,64,256]{2,1,0:T(8,128)(2,1)S(1)} %fusion.246) | copy-start | bytes 1179652
  307.8 117.4 %copy-start = (f32[256,768]{1,0:T(8,128)}, f32[256,768]{1,0:T(8,128)S(1)}, u32[]{:S(2)}) copy-start(f32[256,768]{1,0:T(8,128)S(1)} %get-tuple-element.993) | copy-start | bytes 2359300
  307.8 106.6 %copy-start.51 = (f32[256]{0:T(256)}, f32[256]{0:T(256)S(1)}, u32[]{:S(2)}) copy-start(f32[256]{0:T(256)S(1)} %broadcast_multiply_fusion.1) | copy-start | bytes 3076
  308.0 63.5 %copy-start.61 = (f32[256]{0:T(256)}, f32[256]{0:T(256)S(1)}, u32[]{:S(2)}) copy-start(f32[256]{0:T(256)S(1)} %multiply_reduce_fusion.4) | copy-start | bytes 3076
  308.1 106.3 %copy-start.58 = (f32[256]{0:T(256)}, f32[256]{0:T(256)S(1)}, u32[]{:S(2)}) copy-start(f32[256]{0:T(256)S(1)} %fusion.266) | copy-start | bytes 3076
  371.5 46.9 %copy-start.22 = (bf16[256,3072]{1,0:T(8,128)(2,1)}, bf16[256,3072]{1,0:T(8,128)(2,1)S(1)}, u32[]{:S(2)}) copy-start(bf16[256,3072]{1,0:T(8,128)(2,1)S(1)} %get-tuple-element.911) | copy-start | bytes 4718596
  414.4 6.4 slice-start.6
  437.6 618.4 %reduce-scatter.16.cloned.1.call-start = ((), (), s32[]{:S(2)}) async-start(), calls=%async_computation.18 | async-start | bytes 2506752 | tf_op jit(solution)/shard_map/reduce_scatter | solution.py:307
  440.9 616.7 %reduce-scatter.12.cloned.1.call-start = ((), (), s32[]{:S(2)}) async-start(), calls=%async_computation.16 | async-start | bytes 6684672 | tf_op jit(solution)/shard_map/reduce_scatter | solution.py:305
  472.1 587.2 %reduce-scatter.14.cloned.1.call-start = ((), (), s32[]{:S(2)}) async-start(), calls=%async_computation.17 | async-start | bytes 7520256 | tf_op jit(solution)/shard_map/reduce_scatter | solution.py:306
  477.7 583.3 %reduce-scatter.18.cloned.1.call-start = ((), (), s32[]{:S(2)}) async-start(), calls=%async_computation.19 | async-start | bytes 10027008 | tf_op jit(solution)/shard_map/reduce_scatter | solution.py:308
  484.6 578.2 %reduce-scatter.20.cloned.1.call-start = ((), (), s32[]{:S(2)}) async-start(), calls=%async_computation.20 | async-start | bytes 10027008 | tf_op jit(solution)/shard_map/reduce_scatter | solution.py:309
  491.3 787.4 %reduce-scatter.10.cloned.1.call-start = ((), (), s32[]{:S(2)}) async-start(), calls=%async_computation.15 | async-start | bytes 35651584 | tf_op jit(solution)/shard_map/reduce_scatter | solution.py:304
  492.9 9.2 copy-start.11
  515.9 790.0 %all-reduce.44.cloned.1.call-start = ((), (), s32[]{:S(2)}) async-start(), calls=%async_computation.23 | async-start | bytes 294912 | tf_op jit(solution)/shard_map/psum | solution.py:320
  610.5 7.3 copy-start.78
  676.5 7.3 copy-start.78
  741.9 7.3 copy-start.78
  807.5 7.3 copy-start.78
  873.4 7.3 copy-start.78
  938.9 7.3 copy-start.78
  1005.9 7.3 copy-start.78
  1055.3 322.1 %all-reduce.46.cloned.1.call-start = ((), (), s32[]{:S(2)}) async-start(), calls=%async_computation.24 | async-start | bytes 4620288 | tf_op jit(solution)/shard_map/psum | solution.py:320
  1055.9 389.7 %all-reduce.48.cloned.1.call-start = ((), (), s32[]{:S(2)}) async-start(), calls=%async_computation.25 | async-start | bytes 4259840 | tf_op jit(solution)/shard_map/psum | solution.py:312
  1281.4 259.9 %all-reduce.40.cloned.1.call-start = ((), (), s32[]{:S(2)}) async-start(), calls=%async_computation.21 | async-start | bytes 294912 | tf_op jit(solution)/shard_map/psum | solution.py:319
  1305.9 339.9 %all-reduce.42.cloned.1.call-start = ((), (), s32[]{:S(2)}) async-start(), calls=%async_computation.22 | async-start | bytes 4620288 | tf_op jit(solution)/shard_map/psum | solution.py:319
  1541.3 121.4 %copy-start.71 = (f32[768]{0:T(1024)S(1)}, f32[768]{0:T(1024)}, u32[]{:S(2)}) copy-start(f32[768]{0:T(1024)} %get-tuple-element.1472) | copy-start | bytes 9220
  1541.3 122.0 %copy-start.70 = (f32[768]{0:T(1024)S(1)}, f32[768]{0:T(1024)}, u32[]{:S(2)}) copy-start(f32[768]{0:T(1024)} %get-tuple-element.1473) | copy-start | bytes 9220
  1541.3 122.6 %copy-start.69 = (f32[768]{0:T(1024)S(1)}, f32[768]{0:T(1024)}, u32[]{:S(2)}) copy-start(f32[768]{0:T(1024)} %get-tuple-element.1476) | copy-start | bytes 9220
  1541.3 123.2 %copy-start.68 = (f32[768]{0:T(1024)S(1)}, f32[768]{0:T(1024)}, u32[]{:S(2)}) copy-start(f32[768]{0:T(1024)} %get-tuple-element.1477) | copy-start | bytes 9220
  (253 other events, 650.8 us)
Sparse Core Ops, SparseCore 0:
  10.2 129.5 all-gather.7
  142.1 43.5 all-gather.9
  187.9 45.9 all-gather.11
  239.2 26.2 all-gather.13
  267.6 38.3 all-gather.15
  308.1 52.1 all-gather.17
  362.6 51.7 all-gather.19
  437.7 24.6 reduce-scatter.7
  466.6 62.9 reduce-scatter.15
  533.4 84.2 reduce-scatter.11
  622.2 88.9 reduce-scatter.13
  715.2 110.9 reduce-scatter.17
  830.8 111.1 reduce-scatter.19
  946.2 332.4 reduce-scatter.9
  1283.2 22.6 all-reduce.43
  1309.4 68.0 all-reduce.45
  1381.1 64.4 all-reduce.47
  1450.4 90.8 all-reduce.39
  1545.3 100.4 all-reduce.41
